TPU v7x, 32 devices: a whole 2x2x4 slice. The times are simulated.
32 devices in a mesh: ctx: 16 (over z, x, core), tp: 2 (over y).
Axes of the slice: x: 2, y: 2, z: 4, core: 2. Of those that a mesh axis runs over, the one named last changes fastest.
Arguments:
- token_ids: int32 [8192], P('ctx'), may hold values from 0 to 511
- embed_table: bfloat16 [512, 8192], P(None, 'tp'), may hold values from -81 to 81
- projected_table: bfloat16 [512, 3, 8192], P(None, None, 'tp'), may hold values from -10.5 to 10.5
- feat_one: float32 [3, 3, 8192], P(None, None, 'tp'), may hold values from -3 to 3
- inner_taps: float32 [7, 8192], P(None, 'tp'), may hold values from -2 to 2
- feat_two: float32 [3, 3, 8192], P(None, None, 'tp'), may hold values from -3 to 3
- decay: float32 [8192, 16], P('tp'), may hold values from 3.540039e-05 to 0.03448276
- residue: float32 [8192, 16], P('tp'), may hold values from -0.26261287 to 0.26261287
Outputs:
- stream_out: bfloat16 [8192, 8192], P('ctx', 'tp')
All inputs are finite; a program needn't handle non-finite values.
Results may differ from a plain program's by a relative error of at most 0.0048.
Values may be sent and summed in bfloat16 or wider, within the bound.
A program may use at most 320 MiB of HBM per device.

v0:
```python
import math
import jax
import jax.numpy as jnp
from jax import lax
from jax.sharding import PartitionSpec as P

D = 8192
epsilon = 1e-06
PRECISE = lax.Precision.HIGHEST


def shifted(value, axis, steps):
    count = lax.axis_size(axis)
    first, last = (max(0, -steps), min(count, count - steps))
    return lax.ppermute(value, axis, [(source, source + steps) for source in range(first, last)])


def valid_taps(series, weights):
    tap_count = weights.shape[0]
    out_rows = series.shape[0] - tap_count + 1
    summed = weights[0] * series[tap_count - 1 : tap_count - 1 + out_rows]
    for offset in range(1, tap_count):
        summed = (
            summed
            + weights[offset] * series[tap_count - 1 - offset : tap_count - 1 - offset + out_rows]
        )
    return summed


def look_up(all_ids, embed_table, projected_table):
    vocab_size = embed_table.shape[0]
    one_hot = (all_ids[:, None] == jnp.arange(vocab_size, dtype=jnp.int32)[None, :]).astype(
        jnp.bfloat16
    )
    embedded = jnp.dot(one_hot, embed_table, preferred_element_type=jnp.float32)
    flattened = projected_table.reshape(vocab_size, -1)
    raw_rows = jnp.dot(one_hot, flattened, preferred_element_type=jnp.float32)
    return (embedded, raw_rows.reshape(all_ids.shape[0], 3, -1))


def block_one(raw_rows, embedded, feat_one, inner_taps):
    queries = valid_taps(raw_rows[:, 0], feat_one[:, 0])
    key_rows = valid_taps(raw_rows[:, 1], feat_one[:, 1])
    valued = valid_taps(raw_rows[:, 2], feat_one[:, 2])
    mixture = valid_taps(key_rows * valued, inner_taps)
    out_rows = mixture.shape[0]
    return (embedded + queries[queries.shape[0] - out_rows :] * mixture).astype(jnp.bfloat16)


def split_sizes(length):
    columns = 1
    for divisor in range(1, 129):
        if length % divisor == 0:
            columns = divisor
    return (2 * length // columns, columns)


def fourier_tables(outer_len, columns):
    total_len = outer_len * columns
    rows_k = jnp.arange(outer_len, dtype=jnp.int32)
    rows_q = jnp.arange(columns, dtype=jnp.int32)
    outer_angles = (rows_k[:, None] * rows_k[None, :] % outer_len).astype(jnp.float32) * (
        2.0 * math.pi / outer_len
    )
    col_angles = (rows_q[:, None] * rows_q[None, :] % columns).astype(jnp.float32) * (
        2.0 * math.pi / columns
    )
    tw_angles = (rows_k[:, None] * rows_q[None, :] % total_len).astype(jnp.float32) * (
        2.0 * math.pi / total_len
    )
    return (
        jnp.cos(outer_angles),
        -jnp.sin(outer_angles),
        jnp.cos(col_angles),
        -jnp.sin(col_angles),
        jnp.cos(tw_angles),
        -jnp.sin(tw_angles),
    )


def first_section(table, signal):
    if signal.dtype == jnp.bfloat16:
        upper = table.astype(jnp.bfloat16)
        lower = (table - upper.astype(jnp.float32)).astype(jnp.bfloat16)
        return jnp.einsum(
            "kp,bpq->bkq", upper, signal, preferred_element_type=jnp.float32
        ) + jnp.einsum("kp,bpq->bkq", lower, signal, preferred_element_type=jnp.float32)
    return jnp.einsum("kp,bpq->bkq", table, signal, precision=PRECISE)


def forward_transform(signal, tables):
    outer_re, outer_im, col_re, col_im, tw_re, tw_im = tables
    half_rows = signal.shape[1]
    first_re = first_section(outer_re[:, :half_rows], signal)
    first_im = first_section(outer_im[:, :half_rows], signal)
    turned_re = first_re * tw_re - first_im * tw_im
    turned_im = first_re * tw_im + first_im * tw_re
    out_re = jnp.einsum("bkq,ql->bkl", turned_re, col_re, precision=PRECISE) - jnp.einsum(
        "bkq,ql->bkl", turned_im, col_im, precision=PRECISE
    )
    out_im = jnp.einsum("bkq,ql->bkl", turned_re, col_im, precision=PRECISE) + jnp.einsum(
        "bkq,ql->bkl", turned_im, col_re, precision=PRECISE
    )
    return (out_re, out_im)


def inverse_transform(spec_re, spec_im, tables):
    outer_re, outer_im, col_re, col_im, tw_re, tw_im = tables
    outer_len = outer_re.shape[0]
    total_len = outer_len * col_re.shape[0]
    half_rows = outer_len // 2
    back_re = jnp.einsum("bkl,lq->bkq", spec_re, col_re, precision=PRECISE) + jnp.einsum(
        "bkl,lq->bkq", spec_im, col_im, precision=PRECISE
    )
    back_im = jnp.einsum("bkl,lq->bkq", spec_im, col_re, precision=PRECISE) - jnp.einsum(
        "bkl,lq->bkq", spec_re, col_im, precision=PRECISE
    )
    turn_re = back_re * tw_re + back_im * tw_im
    turn_im = back_im * tw_re - back_re * tw_im
    result = jnp.einsum(
        "pk,bkq->bpq", outer_re[:half_rows], turn_re, precision=PRECISE
    ) + jnp.einsum("pk,bkq->bpq", outer_im[:half_rows], turn_im, precision=PRECISE)
    return result / total_len


def causal_convolve(series, response):
    channels, length = series.shape
    outer_len, columns = split_sizes(length)
    tables = fourier_tables(outer_len, columns)
    half_rows = outer_len // 2
    sig_re, sig_im = forward_transform(series.reshape(channels, half_rows, columns), tables)
    fil_re, fil_im = forward_transform(response.reshape(channels, half_rows, columns), tables)
    prod_re = sig_re * fil_re - sig_im * fil_im
    prod_im = sig_re * fil_im + sig_im * fil_re
    return inverse_transform(prod_re, prod_im, tables).reshape(channels, length)


def mode_response(decay, residue, length, offset):
    positions = jnp.arange(length, dtype=jnp.int32).astype(jnp.float32) + offset

    def add_mode(mode_number, summed):
        decay_col = lax.dynamic_slice_in_dim(decay, mode_number, 1, 1)
        weight_col = lax.dynamic_slice_in_dim(residue, mode_number, 1, 1)
        return summed + weight_col * jnp.exp(-decay_col * positions[None, :])

    return lax.fori_loop(
        0, decay.shape[1], add_mode, jnp.zeros((decay.shape[0], length), jnp.float32)
    )


def on_device(
    token_ids, embed_table, projected_table, feat_one, inner_taps, feat_two, decay, residue
):
    tok_rows = token_ids.shape[0]
    channels = embed_table.shape[1]
    lead_one = feat_one.shape[0] - 1 + inner_taps.shape[0] - 1
    lead_two = feat_two.shape[0] - 1
    embedded, raw_rows = look_up(token_ids, embed_table, projected_table)
    raw_sent = raw_rows[tok_rows - lead_one :].astype(jnp.bfloat16)
    earlier = shifted(raw_sent, "ctx", 1)
    raw_ext = jnp.concatenate([earlier.astype(jnp.float32), raw_rows], axis=0)
    stream = block_one(raw_ext, embedded, feat_one, inner_taps)
    before = shifted(stream[tok_rows - lead_two :], "ctx", 1)
    stream_ext = jnp.concatenate([before, stream], axis=0)
    widened = stream_ext.astype(jnp.float32)
    squares = lax.psum(jnp.sum(widened * widened, axis=1), "tp")
    normed = widened * lax.rsqrt(squares / D + epsilon)[:, None]
    queries = valid_taps(normed, feat_two[:, 0])
    key_rows = valid_taps(normed, feat_two[:, 1])
    valued = valid_taps(normed, feat_two[:, 2])
    product = jnp.transpose(key_rows * valued).astype(jnp.bfloat16)
    per_device = channels // lax.axis_size("ctx")
    gathered = lax.all_to_all(product, "ctx", split_axis=0, concat_axis=1, tiled=True)
    first_lane = lax.axis_index("ctx") * per_device
    my_decay = lax.dynamic_slice_in_dim(decay, first_lane, per_device, 0)
    my_residue = lax.dynamic_slice_in_dim(residue, first_lane, per_device, 0)
    response = mode_response(my_decay, my_residue, gathered.shape[1], 0.0)
    convolved = causal_convolve(gathered, response)
    carried = lax.all_to_all(convolved, "ctx", split_axis=1, concat_axis=0, tiled=True)
    mixed_out = queries * jnp.transpose(carried)
    return (widened[lead_two:] + mixed_out).astype(jnp.bfloat16)


def solution(mesh):
    placed = (
        P("ctx"),
        P(None, "tp"),
        P(None, None, "tp"),
        P(None, None, "tp"),
        P(None, "tp"),
        P(None, None, "tp"),
        P("tp", None),
        P("tp", None),
    )
    return jax.shard_map(
        on_device, mesh=mesh, in_specs=placed, out_specs=P("ctx", "tp"), check_vma=False
    )
```

profile of v0, /device:TPU:15, one launch (start us, length us, event | category | flops | bytes accessed | tf_op | source)
XLA Modules:
  0.0 1082.3 jit_solution(17847357074202862382)
XLA Ops:
  16.7 20.7 %fusion.72 = f32[512,12288]{1,0:T(8,128)} fusion(bf16[512,12288]{0,1:T(8,128)(2,1)} %bitcast.240, s32[512]{0:T(512)S(1)} %copy-done.9), kind=kOutput, calls=%fused_computation.119 | convolution fusion | flops 6442713088 | bytes 37750784 | tf_op jit(solution)/shard_map/dot_general | solution.py:37
  44.1 100.5 %while.14 = (s32[]{:T(128)}, f32[256,8192]{1,0:T(8,128)}, f32[256,16]{0,1:T(8,128)S(1)}, f32[256,16]{0,1:T(8,128)S(1)}, s32[]{:T(128)}, /*index=5*/s32[]{:T(128)}) while((s32[]{:T(128)}, f32[256,8192]{1,0:T(8,128)}, f32[256,16]{0,1:T(8,128)S(1)}, f32[256,16]{0,1:T(8,128)S(1)}, s32[]{:T(128)}, /*index=5*/s32[]{:T(128)}) %tuple.64), condition=%wide.region_3.0_spmd.clone, body=%wide.region_2.0_spmd.clone.sunk | while | flops 8397059 | bytes 16848984 | solution.py:146
  152.9 29.2 %fusion.100 = f32[256,128,128]{2,1,0:T(8,128)} fusion(f32[256,64,128]{2,1,0:T(8,128)S(1)} %bitcast.238, f32[128,128]{0,1:T(8,128)S(1)} %sine_negate_fusion.1), kind=kOutput, calls=%fused_computation.158 | convolution fusion | flops 3221225472 | bytes 25198592 | tf_op jit(solution)/shard_map/kp,bpq->bkq/dot_general | solution.py:88
  182.1 24.7 %copy.73 = f32[512,12288]{0,1:T(8,128)} copy(f32[512,12288]{1,0:T(8,128)} %fusion.72) | data formatting | bytes 50331648 | tf_op jit(solution)/shard_map/dot_general | solution.py:37
  206.8 25.0 %copy.74 = f32[512,3,4096]{2,0,1:T(8,128)} copy(f32[512,3,4096]{0,2,1:T(8,128)} %bitcast.241) | data formatting | bytes 50331648 | tf_op jit(solution)/shard_map/reshape | solution.py:38
  250.2 21.3 %fusion.19 = f32[518,4096]{1,0:T(8,128)} fusion(f32[512,3,4096]{2,0,1:T(8,128)} %copy.74, f32[8,3,4096]{2,0,1:T(8,128)S(1)} %convert_element_type.123, f32[4096]{0:T(1024)S(1)} %bitcast.253, f32[4096]{0:T(1024)S(1)} %bitcast.254, f32[4096]{0:T(1024)S(1)} %bitcast.249, f32[4096]{0:T(1024)S(1)} %bitcast.250, f32[4096]{0:T(1024)S(1)} %bitcast.251, ...), kind=kLoop, calls=%fused_computation.56 | loop fusion | flops 36069376 | bytes 34144256 | tf_op jit(solution)/shard_map/mul | solution.py:45
  271.5 36.9 %fusion.46 = bf16[512,4096]{1,0:T(8,128)(2,1)} fusion(f32[518,4096]{1,0:T(8,128)} %fusion.19, f32[518,4096]{1,0:T(8,128)} %get-tuple-element.130, f32[518,4096]{1,0:T(8,128)} %get-tuple-element.131, f32[518,4096]{1,0:T(8,128)} %get-tuple-element.129, bf16[512,4096]{1,0:T(8,128)(2,1)} %param.11, f32[4096]{0:T(1024)S(1)} %bitcast.272, ...), kind=kOutput, calls=%fused_computation.87 | convolution fusion | flops 2191785984 | bytes 92440576 | tf_op jit(solution)/shard_map/dot_general | solution.py:35
  339.0 30.5 %fusion.102 = f32[256,128,128]{2,1,0:T(8,128)} fusion(f32[256,64,128]{2,1,0:T(8,128)} %bitcast.239, f32[128,128]{0,1:T(8,128)S(1)} %fusion.105), kind=kOutput, calls=%fused_computation.160 | convolution fusion | flops 3221225472 | bytes 25198592 | tf_op jit(solution)/shard_map/kp,bpq->bkq/dot_general | solution.py:88
  369.5 32.9 %fusion.66 = f32[256,128,128]{2,1,0:T(8,128)} fusion(f32[256,128,128]{2,1,0:T(8,128)S(1)} %bitcast.236, f32[256,128,128]{2,1,0:T(8,128)} %fusion.102, f32[128,128]{0,1:T(8,128)S(1)} %get-tuple-element.159, f32[128,128]{0,1:T(8,128)S(1)} %get-tuple-element.160), kind=kOutput, calls=%fused_computation.113 | convolution fusion | flops 6455279616 | bytes 50462720 | tf_op jit(solution)/shard_map/bkq,ql->bkl/dot_general | solution.py:101
  402.4 33.1 %fusion.68 = f32[256,128,128]{2,1,0:T(8,128)} fusion(f32[256,128,128]{2,1,0:T(8,128)S(1)} %bitcast.236, f32[256,128,128]{2,1,0:T(8,128)} %fusion.102, f32[128,128]{0,1:T(8,128)S(1)} %get-tuple-element.159, f32[128,128]{0,1:T(8,128)S(1)} %get-tuple-element.160), kind=kOutput, calls=%fused_computation.114 | convolution fusion | flops 6455263232 | bytes 50462720 | tf_op jit(solution)/shard_map/bkq,ql->bkl/dot_general | solution.py:98
  435.5 34.1 %convolution_add_fusion.3 = f32[256,128,128]{2,1,0:T(8,128)} fusion(f32[256,128,128]{2,1,0:T(8,128)} %fusion.66, f32[256,128,128]{2,1,0:T(8,128)S(1)} %bitcast.236, f32[256,128,128]{2,1,0:T(8,128)} %fusion.102, f32[128,128]{0,1:T(8,128)S(1)} %get-tuple-element.159, f32[128,128]{0,1:T(8,128)S(1)} %get-tuple-element.160), kind=kOutput, calls=%fused_computation.47 | convolution fusion | flops 6459457536 | bytes 67239936 | tf_op jit(solution)/shard_map/bkq,ql->bkl/dot_general | solution.py:101
  469.6 34.1 %convolution_subtract_fusion.1 = f32[256,128,128]{2,1,0:T(8,128)} fusion(f32[256,128,128]{2,1,0:T(8,128)} %fusion.68, f32[256,128,128]{2,1,0:T(8,128)S(1)} %bitcast.236, f32[256,128,128]{2,1,0:T(8,128)} %fusion.102, f32[128,128]{0,1:T(8,128)S(1)} %get-tuple-element.159, f32[128,128]{0,1:T(8,128)S(1)} %get-tuple-element.160), kind=kOutput, calls=%fused_computation.49 | convolution fusion | flops 6459473920 | bytes 67239936 | tf_op jit(solution)/shard_map/bkq,ql->bkl/dot_general | solution.py:98
  537.7 21.2 %convolution_add_fusion.1 = f32[256,128,128]{2,1,0:T(8,128)} fusion(f32[256,128,128]{2,1,0:T(8,128)} %fusion.120, bf16[256,64,128]{2,1,0:T(8,128)(2,1)} %copy.135, f32[128,128]{0,1:T(8,128)S(1)} %fusion.105), kind=kOutput, calls=%fused_computation.44 | convolution fusion | flops 541097984 | bytes 37781504 | tf_op jit(solution)/shard_map/kp,bpq->bkq/dot_general | solution.py:87
  558.9 32.6 %fusion.60 = f32[256,128,128]{2,1,0:T(8,128)} fusion(f32[256,128,128]{2,1,0:T(8,128)S(1)} %convolution_add_fusion, f32[256,128,128]{2,1,0:T(8,128)} %convolution_add_fusion.1, f32[128,128]{0,1:T(8,128)S(1)} %get-tuple-element.159, f32[128,128]{0,1:T(8,128)S(1)} %get-tuple-element.160), kind=kOutput, calls=%fused_computation.111 | convolution fusion | flops 6455279616 | bytes 50462720 | tf_op jit(solution)/shard_map/bkq,ql->bkl/dot_general | solution.py:101
  591.5 32.8 %fusion.62 = f32[256,128,128]{2,1,0:T(8,128)} fusion(f32[256,128,128]{2,1,0:T(8,128)S(1)} %convolution_add_fusion, f32[256,128,128]{2,1,0:T(8,128)} %convolution_add_fusion.1, f32[128,128]{0,1:T(8,128)S(1)} %get-tuple-element.159, f32[128,128]{0,1:T(8,128)S(1)} %get-tuple-element.160), kind=kOutput, calls=%fused_computation.112 | convolution fusion | flops 6455263232 | bytes 50462720 | tf_op jit(solution)/shard_map/bkq,ql->bkl/dot_general | solution.py:98
  624.3 34.1 %convolution_subtract_fusion.2 = f32[256,128,128]{2,1,0:T(8,128)} fusion(f32[256,128,128]{2,1,0:T(8,128)} %fusion.62, f32[256,128,128]{2,1,0:T(8,128)S(1)} %convolution_add_fusion, f32[256,128,128]{2,1,0:T(8,128)} %convolution_add_fusion.1, f32[128,128]{0,1:T(8,128)S(1)} %get-tuple-element.159, f32[128,128]{0,1:T(8,128)S(1)} %get-tuple-element.160), kind=kOutput, calls=%fused_computation.50 | convolution fusion | flops 6459473920 | bytes 67239936 | tf_op jit(solution)/shard_map/bkq,ql->bkl/dot_general | solution.py:98
  658.4 51.1 %multiply_add_fusion = (f32[256,128,128]{2,1,0:T(8,128)}, f32[256,128,128]{2,1,0:T(8,128)}) fusion(f32[256,128,128]{2,1,0:T(8,128)} %convolution_subtract_fusion.1, f32[256,128,128]{2,1,0:T(8,128)} %convolution_subtract_fusion.2, f32[256,128,128]{2,1,0:T(8,128)} %convolution_add_fusion.3, f32[256,128,128]{2,1,0:T(8,128)} %fusion.60, ...), kind=kOutput, calls=%fused_computation.33 | convolution fusion | flops 6484623360 | bytes 134348800 | tf_op jit(solution)/shard_map/bkq,ql->bkl/dot_general | solution.py:101
  709.4 23.2 %fusion.85 = f32[256,128,128]{1,2,0:T(8,128)} fusion(f32[256,128,128]{2,1,0:T(8,128)} %get-tuple-element.127), kind=kOutput, calls=%fused_computation.140 | convolution fusion | flops 6442680320 | bytes 33554432 | tf_op jit(solution)/shard_map/bkl,lq->bkq/dot_general | solution.py:115
  732.7 22.9 %fusion.87 = f32[256,128,128]{1,2,0:T(8,128)} fusion(f32[256,128,128]{2,1,0:T(8,128)} %get-tuple-element.128), kind=kOutput, calls=%fused_computation.142 | convolution fusion | flops 6442680320 | bytes 33554432 | tf_op jit(solution)/shard_map/bkl,lq->bkq/dot_general | solution.py:112
  755.6 24.0 %convolution_subtract_fusion = f32[256,128,128]{1,2,0:T(8,128)} fusion(f32[256,128,128]{1,2,0:T(8,128)} %fusion.85, f32[256,128,128]{2,1,0:T(8,128)} %get-tuple-element.128), kind=kOutput, calls=%fused_computation.45 | convolution fusion | flops 6446891008 | bytes 50331648 | tf_op jit(solution)/shard_map/bkl,lq->bkq/dot_general | solution.py:115
  779.6 23.9 %convolution_add_fusion.2 = f32[256,128,128]{1,2,0:T(8,128)} fusion(f32[256,128,128]{1,2,0:T(8,128)} %fusion.87, f32[256,128,128]{2,1,0:T(8,128)} %get-tuple-element.127), kind=kOutput, calls=%fused_computation.46 | convolution fusion | flops 6446891008 | bytes 50331648 | tf_op jit(solution)/shard_map/bkl,lq->bkq/dot_general | solution.py:112
  803.4 28.4 %fusion.6 = f32[256,128,64]{1,2,0:T(8,128)} fusion(f32[256,128,128]{1,2,0:T(8,128)} %convolution_add_fusion.2, f32[256,128,128]{1,2,0:T(8,128)} %convolution_subtract_fusion, f32[128,128]{0,1:T(8,128)S(1)} %get-tuple-element.159, f32[128,128]{0,1:T(8,128)S(1)} %get-tuple-element.160, f32[128,128]{0,1:T(8,128)S(1)} %copy-done.6), kind=kOutput, calls=%fused_computation.25 | convolution fusion | flops 3233808384 | bytes 42139648 | tf_op jit(solution)/shard_map/pk,bkq->bpq/dot_general | solution.py:122
  831.9 26.7 %multiply_bitcast_fusion = f32[256,64,128]{2,1,0:T(8,128)} fusion(f32[256,128,64]{1,2,0:T(8,128)} %fusion.6, f32[256,128,128]{1,2,0:T(8,128)} %convolution_subtract_fusion, f32[256,128,128]{1,2,0:T(8,128)} %convolution_add_fusion.2, f32[128,128]{0,1:T(8,128)S(1)} %get-tuple-element.159, f32[128,128]{0,1:T(8,128)S(1)} %get-tuple-element.160, ...), kind=kOutput, calls=%fused_computation.105 | convolution fusion | flops 3238002688 | bytes 50528256 | tf_op jit(solution)/shard_map/pk,bkq->bpq/dot_general | solution.py:120
  880.7 175.6 %all-to-all-done.1 = f32[256,16,512]{0,2,1:T(8,128)} async-done(((f32[256,16,512]{0,2,1:T(8,128)}), f32[256,16,512]{0,2,1:T(8,128)}, u32[]{:S(2)}, u32[]{:S(2)}) %all-to-all-start.1) | async-done | bytes 8388640 | tf_op jit(solution)/shard_map/all_to_all | solution.py:179
  (128 shorter events, 262.3 us)
Async XLA Ops:
  0.0 16.6 %copy-start.9 = (s32[512]{0:T(512)S(1)}, s32[512]{0:T(512)}, u32[]{:S(2)}) copy-start(s32[512]{0:T(512)} %param.10) | copy-start | bytes 6148
  16.6 25.8 %copy-start.14 = (f32[7,4096]{1,0:T(8,128)S(1)}, f32[7,4096]{1,0:T(8,128)}, u32[]{:S(2)}) copy-start(f32[7,4096]{1,0:T(8,128)} %param.14) | copy-start | bytes 344068
  16.6 25.9 %copy-start.12 = (f32[3,3,4096]{2,1,0:T(4,128)S(1)}, f32[3,3,4096]{2,1,0:T(4,128)}, u32[]{:S(2)}) copy-start(f32[3,3,4096]{2,1,0:T(4,128)} %param.13) | copy-start | bytes 442372
  16.7 26.0 %copy-start.13 = (f32[3,3,4096]{2,1,0:T(4,128)S(1)}, f32[3,3,4096]{2,1,0:T(4,128)}, u32[]{:S(2)}) copy-start(f32[3,3,4096]{2,1,0:T(4,128)} %param.15) | copy-start | bytes 442372
  38.4 193.4 %collective-permute-start = (bf16[8,3,4096]{2,0,1:T(8,128)(2,1)S(1)}, bf16[8,3,4096]{2,0,1:T(8,128)(2,1)S(1)}, u32[]{:S(2)}, u32[]{:S(2)}) collective-permute-start(bf16[8,3,4096]{2,0,1:T(8,128)(2,1)S(1)} %bitcast.246), channel_id=1, source_target_pairs={{0,2},{2,4},{4,6},{6,8},{8,10},{10,12},{12,14},{14,16},{16,18},{18... | collective-permute-start | bytes 589832 | tf_op jit(solution)/shard_map/ppermute | solution.py:15
  42.4 107.2 %copy-start.4 = (f32[128,128]{0,1:T(8,128)}, f32[128,128]{0,1:T(8,128)S(1)}, u32[]{:S(2)}) copy-start(f32[128,128]{0,1:T(8,128)S(1)} %sine_negate_fusion.1) | copy-start | bytes 196612
  309.3 3.1 collective-permute-start.1
  312.4 16.1 %copy-start.10 = (bf16[2,4096]{1,0:T(2,128)(2,1)}, bf16[2,4096]{1,0:T(2,128)(2,1)S(1)}, u32[]{:S(2)}) copy-start(bf16[2,4096]{1,0:T(2,128)(2,1)S(1)} %collective-permute-done.1) | copy-start | bytes 49156
  330.9 172.8 %all-to-all-start = ((bf16[16,256,512]{1,2,0:T(8,128)(2,1)}), bf16[16,256,512]{1,2,0:T(8,128)(2,1)}, u32[]{:S(2)}, u32[]{:S(2)}) async-start(bf16[16,256,512]{1,2,0:T(8,128)(2,1)} %bitcast.244), calls=%async_computation | async-start | bytes 8388608 | tf_op jit(solution)/shard_map/all_to_all | solution.py:173
  338.7 30.8 %slice-start = ((s8[16777216]{0:T(1024)(128)(4,1)}), s8[4194304]{0:T(1024)(128)(4,1)S(1)}, s32[]{:S(2)}) async-start(s8[16777216]{0:T(1024)(128)(4,1)} %bitcast.235), calls=%async_computation.2 | async-start | bytes 8388608
  339.0 198.7 %copy-start.7 = (f32[128,128]{0,1:T(8,128)}, f32[128,128]{0,1:T(8,128)S(1)}, u32[]{:S(2)}) copy-start(f32[128,128]{0,1:T(8,128)S(1)} %fusion.105) | copy-start | bytes 196612
  339.0 30.5 %slice-start.1 = ((s8[16777216]{0:T(1024)(128)(4,1)}), s8[4194304]{0:T(1024)(128)(4,1)S(1)}, s32[]{:S(2)}) async-start(s8[16777216]{0:T(1024)(128)(4,1)} %bitcast.235), calls=%async_computation.3 | async-start | bytes 8388608
  339.0 30.5 %slice-start.2 = ((s8[16777216]{0:T(1024)(128)(4,1)}), s8[4194304]{0:T(1024)(128)(4,1)S(1)}, s32[]{:S(2)}) async-start(s8[16777216]{0:T(1024)(128)(4,1)} %bitcast.235), calls=%async_computation.4 | async-start | bytes 8388608
  339.0 30.5 %slice-start.3 = ((s8[16777216]{0:T(1024)(128)(4,1)}), s8[4194304]{0:T(1024)(128)(4,1)S(1)}, s32[]{:S(2)}) async-start(s8[16777216]{0:T(1024)(128)(4,1)} %bitcast.235), calls=%async_computation.5 | async-start | bytes 8388608
  469.6 40.7 %copy-start.5 = (f32[128,128]{0,1:T(8,128)S(1)}, f32[128,128]{0,1:T(8,128)}, u32[]{:S(2)}) copy-start(f32[128,128]{0,1:T(8,128)} %copy-done.4) | copy-start | bytes 196612
  510.3 10.5 copy-start.2
  537.7 86.6 %copy-start = (f32[256,128,128]{2,1,0:T(8,128)}, f32[256,128,128]{2,1,0:T(8,128)S(1)}, u32[]{:S(2)}) copy-start(f32[256,128,128]{2,1,0:T(8,128)S(1)} %convolution_add_fusion) | copy-start | bytes 50331652
  779.6 23.9 %copy-start.6 = (f32[128,128]{0,1:T(8,128)S(1)}, f32[128,128]{0,1:T(8,128)}, u32[]{:S(2)}) copy-start(f32[128,128]{0,1:T(8,128)} %copy-done.4) | copy-start | bytes 196612
  803.4 28.4 %copy-start.8 = (f32[128,128]{0,1:T(8,128)S(1)}, f32[128,128]{0,1:T(8,128)}, u32[]{:S(2)}) copy-start(f32[128,128]{0,1:T(8,128)} %copy-done.7) | copy-start | bytes 196612
  867.8 6.2 copy-start.11
  867.8 188.5 %all-to-all-start.1 = ((f32[256,16,512]{0,2,1:T(8,128)}), f32[256,16,512]{0,2,1:T(8,128)}, u32[]{:S(2)}, u32[]{:S(2)}) async-start(f32[256,16,512]{0,2,1:T(8,128)} %bitcast.242), calls=%async_computation.1 | async-start | bytes 16777216 | tf_op jit(solution)/shard_map/all_to_all | solution.py:179
  880.7 183.4 %copy-start.15 = (f32[1,1,4096]{2,1,0:T(1,128)S(1)}, f32[1,1,4096]{2,1,0:T(1,128)}, u32[]{:S(2)}) copy-start(f32[1,1,4096]{2,1,0:T(1,128)} %get-tuple-element.132) | copy-start | bytes 49156
  880.7 183.4 %copy-start.16 = (f32[1,1,4096]{2,1,0:T(1,128)S(1)}, f32[1,1,4096]{2,1,0:T(1,128)}, u32[]{:S(2)}) copy-start(f32[1,1,4096]{2,1,0:T(1,128)} %get-tuple-element.137) | copy-start | bytes 49156
  880.7 183.4 %copy-start.17 = (f32[1,1,4096]{2,1,0:T(1,128)S(1)}, f32[1,1,4096]{2,1,0:T(1,128)}, u32[]{:S(2)}) copy-start(f32[1,1,4096]{2,1,0:T(1,128)} %get-tuple-element.138) | copy-start | bytes 49156
  (2 other events, 7.8 us)
where the time goes:
time: 1090 us; the launch traced here: 1080 us
  matrix products  600 us (55%)
  other arithmetic  177 us (16%)
  waiting for transfers between devices  176 us (16%)
  local copies, waits for them, and re-layouts  104 us (10%)
  starting transfers between devices  19.6 us (2%)
    all_to_all x1, waiting for transfers between devices, on_device(): lax.all_to_all(convolved, 'ctx', split_axis=1, concat_axis=0, tiled=True)  176 us
    add x16, other arithmetic, add_mode(): return summed + weight_col * jnp.exp(-decay_col * positions[None, :])  99.6 us
    dot_general x2, matrix products, forward_transform(): jnp.einsum('bkq,ql->bkl', turned_im, col_re, precision=PRECISE)  85.2 us
    dot_general x2, matrix products, forward_transform(): jnp.einsum('bkq,ql->bkl', turned_im, col_im, precision=PRECISE)  68.2 us
    dot_general x2, matrix products, forward_transform(): jnp.einsum('bkq,ql->bkl', turned_re, col_re, precision=PRECISE)  65.9 us
    dot_general x2, matrix products, forward_transform(): jnp.einsum('bkq,ql->bkl', turned_re, col_im, precision=PRECISE)  65.4 us
    dot_general x2, matrix products, first_section(): return jnp.einsum('kp,bpq->bkq', table, signal, precision=PRECISE)  59.7 us
    dot_general x1, matrix products, look_up(): embedded = jnp.dot(one_hot, embed_table, preferred_element_type=jnp.float32)  36.9 us
  transfers between devices with their start and end apart: 4, of which 2 were waited for; matrix products, arithmetic and copies ran while one was open for 33% of the time, Pallas kernels for 0%

commit v1 on v0

--- a/solution.py
+++ b/solution.py
@@ -7,6 +7,29 @@
 D = 8192
 epsilon = 1e-06
 PRECISE = lax.Precision.HIGHEST
+
+
+def split_up(value, dim, length):
+    shape = value.shape
+    blocks = value.reshape(*shape[:dim], length, shape[dim] // length, *shape[dim + 1 :])
+    return jnp.moveaxis(blocks, dim, 0)
+
+
+def laid_out(blocks, dim):
+    blocks = jnp.moveaxis(blocks, 0, dim)
+    dims = blocks.shape
+    return blocks.reshape(*dims[:dim], dims[dim] * dims[dim + 1], *dims[dim + 2 :])
+
+
+def exchange_directly(value, axis, split_dim, concat_dim):
+    count, position = (lax.axis_size(axis), lax.axis_index(axis))
+    blocks = split_up(value, split_dim, count)
+    done = [blocks[position]]
+    for lap in range(1, count):
+        sent = blocks[(position + lap) % count]
+        done.append(lax.ppermute(sent, axis, [(i, (i + lap) % count) for i in range(count)]))
+    blocks = jnp.stack(done)[(position - jnp.arange(count)) % count]
+    return laid_out(blocks, concat_dim)
 
 
 def shifted(value, axis, steps):
@@ -176,7 +199,7 @@
     my_residue = lax.dynamic_slice_in_dim(residue, first_lane, per_device, 0)
     response = mode_response(my_decay, my_residue, gathered.shape[1], 0.0)
     convolved = causal_convolve(gathered, response)
-    carried = lax.all_to_all(convolved, "ctx", split_axis=1, concat_axis=0, tiled=True)
+    carried = exchange_directly(convolved, "ctx", 1, 0)
     mixed_out = queries * jnp.transpose(carried)
     return (widened[lead_two:] + mixed_out).astype(jnp.bfloat16)
 

time: 1090 us -> 1150 us (1.055)
  local copies, waits for them, and re-layouts: 104 us -> 160 us
    all_to_all x1 -> x0, waiting for transfers between devices: 176 us -> none  [on_device(): lax.all_to_all(convolved, 'ctx', split_axis=1, concat_axis=0, tiled=True)]
    ppermute x0 -> x15, waiting for transfers between devices: none -> 170 us  [exchange_directly(): lax.ppermute(sent, axis, [(i, (i + lap) % count) for i in range(count)])]
    another operation x0 -> x3, local copies, waits for them, and re-layouts: none -> 40.3 us
    all_to_all x2 -> x0, local copies, waits for them, and re-layouts: 17.1 us -> none  [on_device(): lax.all_to_all(convolved, 'ctx', split_axis=1, concat_axis=0, tiled=True)]
    unnamed x46 -> x102, local copies, waits for them, and re-layouts: 25 us -> 40.5 us
  transfers between devices with their start and end apart: 4 -> 18, of which waited for: 2 -> 10; matrix products, arithmetic and copies ran while one was open for 33% -> 33% of each run, Pallas kernels for 0% -> 0%
where the time goes in v1:
time: 1150 us; the launch traced here: 1140 us
  matrix products  606 us (53%)
  other arithmetic  176 us (15%)
  waiting for transfers between devices  170 us (15%)
  local copies, waits for them, and re-layouts  160 us (14%)
  starting transfers between devices  24.4 us (2%)
    ppermute x15, waiting for transfers between devices, exchange_directly(): lax.ppermute(sent, axis, [(i, (i + lap) % count) for i in range(count)])  170 us
    add x16, other arithmetic, add_mode(): return summed + weight_col * jnp.exp(-decay_col * positions[None, :])  100 us
    dot_general x2, matrix products, forward_transform(): jnp.einsum('bkq,ql->bkl', turned_im, col_re, precision=PRECISE)  85.2 us
    dot_general x2, matrix products, forward_transform(): jnp.einsum('bkq,ql->bkl', turned_im, col_im, precision=PRECISE)  68.2 us
    dot_general x2, matrix products, forward_transform(): jnp.einsum('bkq,ql->bkl', turned_re, col_im, precision=PRECISE)  66.6 us
    dot_general x2, matrix products, forward_transform(): jnp.einsum('bkq,ql->bkl', turned_re, col_re, precision=PRECISE)  65.9 us
    dot_general x2, matrix products, first_section(): return jnp.einsum('kp,bpq->bkq', table, signal, precision=PRECISE)  60.8 us
    unnamed x102, local copies, waits for them, and re-layouts  40.5 us
  transfers between devices with their start and end apart: 18, of which 10 were waited for; matrix products, arithmetic and copies ran while one was open for 33% of the time, Pallas kernels for 0%

profile of v1, /device:TPU:15, one launch (start us, length us, event | category | flops | bytes accessed | tf_op | source)
XLA Modules:
  0.0 1141.7 jit_solution(2019299401036185639)
XLA Ops:
  43.8 24.8 %copy.72 = f32[512,12288]{0,1:T(8,128)} copy(f32[512,12288]{1,0:T(8,128)} %fusion.72) | data formatting | bytes 50331648 | tf_op jit(solution)/shard_map/dot_general | solution.py:60
  70.3 100.4 %while.14 = (s32[]{:T(128)}, f32[256,8192]{1,0:T(8,128)}, f32[256,16]{0,1:T(8,128)S(1)}, f32[256,16]{0,1:T(8,128)S(1)}, s32[]{:T(128)}, /*index=5*/s32[]{:T(128)}) while((s32[]{:T(128)}, f32[256,8192]{1,0:T(8,128)}, f32[256,16]{0,1:T(8,128)S(1)}, f32[256,16]{0,1:T(8,128)S(1)}, s32[]{:T(128)}, /*index=5*/s32[]{:T(128)}) %tuple.79), condition=%wide.region_3.0_spmd.clone, body=%wide.region_2.0_spmd.clone.sunk | while | flops 8397059 | bytes 16848984 | solution.py:169
  179.1 25.1 %copy.73 = f32[512,3,4096]{2,0,1:T(8,128)} copy(f32[512,3,4096]{0,2,1:T(8,128)} %bitcast.317) | data formatting | bytes 50331648 | tf_op jit(solution)/shard_map/reshape | solution.py:61
  204.2 30.3 %fusion.100 = f32[256,128,128]{2,1,0:T(8,128)} fusion(f32[256,64,128]{2,1,0:T(8,128)} %bitcast.314, f32[128,128]{0,1:T(8,128)S(1)} %sine_negate_fusion.1), kind=kOutput, calls=%fused_computation.190 | convolution fusion | flops 3221225472 | bytes 25198592 | tf_op jit(solution)/shard_map/kp,bpq->bkq/dot_general | solution.py:111
  252.9 21.2 %fusion.19 = f32[518,4096]{1,0:T(8,128)} fusion(f32[512,3,4096]{2,0,1:T(8,128)} %copy.73, f32[8,3,4096]{2,0,1:T(8,128)S(1)} %convert_element_type.123, f32[4096]{0:T(1024)S(1)} %bitcast.343, f32[4096]{0:T(1024)S(1)} %bitcast.344, f32[4096]{0:T(1024)S(1)} %bitcast.339, f32[4096]{0:T(1024)S(1)} %bitcast.340, f32[4096]{0:T(1024)S(1)} %bitcast.341, ...), kind=kLoop, calls=%fused_computation.57 | loop fusion | flops 36069376 | bytes 34144256 | tf_op jit(solution)/shard_map/mul | solution.py:68
  274.1 39.9 %fusion.46 = bf16[512,4096]{1,0:T(8,128)(2,1)} fusion(f32[518,4096]{1,0:T(8,128)} %fusion.19, f32[518,4096]{1,0:T(8,128)} %get-tuple-element.130, f32[518,4096]{1,0:T(8,128)} %get-tuple-element.131, f32[518,4096]{1,0:T(8,128)} %get-tuple-element.129, bf16[512,4096]{1,0:T(8,128)(2,1)} %param.11, f32[4096]{0:T(1024)S(1)} %bitcast.362, ...), kind=kOutput, calls=%fused_computation.88 | convolution fusion | flops 2191785984 | bytes 92440576 | tf_op jit(solution)/shard_map/dot_general | solution.py:58
  344.4 30.5 %fusion.102 = f32[256,128,128]{2,1,0:T(8,128)} fusion(f32[256,64,128]{2,1,0:T(8,128)} %bitcast.315, f32[128,128]{0,1:T(8,128)S(1)} %copy-done.17), kind=kOutput, calls=%fused_computation.192 | convolution fusion | flops 3221225472 | bytes 25198592 | tf_op jit(solution)/shard_map/kp,bpq->bkq/dot_general | solution.py:111
  374.9 34.1 %fusion.66 = f32[256,128,128]{2,1,0:T(8,128)} fusion(f32[256,128,128]{2,1,0:T(8,128)} %fusion.100, f32[256,128,128]{2,1,0:T(8,128)} %fusion.102, f32[128,128]{0,1:T(8,128)S(1)} %get-tuple-element.175, f32[128,128]{0,1:T(8,128)S(1)} %get-tuple-element.176), kind=kOutput, calls=%fused_computation.114 | convolution fusion | flops 6455279616 | bytes 50462720 | tf_op jit(solution)/shard_map/bkq,ql->bkl/dot_general | solution.py:124
  409.0 33.1 %fusion.68 = f32[256,128,128]{2,1,0:T(8,128)} fusion(f32[256,128,128]{2,1,0:T(8,128)S(1)} %bitcast.312, f32[256,128,128]{2,1,0:T(8,128)} %fusion.102, f32[128,128]{0,1:T(8,128)S(1)} %get-tuple-element.175, f32[128,128]{0,1:T(8,128)S(1)} %get-tuple-element.176), kind=kOutput, calls=%fused_computation.115 | convolution fusion | flops 6455263232 | bytes 50462720 | tf_op jit(solution)/shard_map/bkq,ql->bkl/dot_general | solution.py:121
  442.1 34.1 %convolution_add_fusion.3 = f32[256,128,128]{2,1,0:T(8,128)} fusion(f32[256,128,128]{2,1,0:T(8,128)} %fusion.66, f32[256,128,128]{2,1,0:T(8,128)S(1)} %bitcast.312, f32[256,128,128]{2,1,0:T(8,128)} %fusion.102, f32[128,128]{0,1:T(8,128)S(1)} %get-tuple-element.175, f32[128,128]{0,1:T(8,128)S(1)} %get-tuple-element.176), kind=kOutput, calls=%fused_computation.48 | convolution fusion | flops 6459457536 | bytes 67239936 | tf_op jit(solution)/shard_map/bkq,ql->bkl/dot_general | solution.py:124
  476.2 34.1 %convolution_subtract_fusion.1 = f32[256,128,128]{2,1,0:T(8,128)} fusion(f32[256,128,128]{2,1,0:T(8,128)} %fusion.68, f32[256,128,128]{2,1,0:T(8,128)S(1)} %bitcast.312, f32[256,128,128]{2,1,0:T(8,128)} %fusion.102, f32[128,128]{0,1:T(8,128)S(1)} %get-tuple-element.175, f32[128,128]{0,1:T(8,128)S(1)} %get-tuple-element.176), kind=kOutput, calls=%fused_computation.50 | convolution fusion | flops 6459473920 | bytes 67239936 | tf_op jit(solution)/shard_map/bkq,ql->bkl/dot_general | solution.py:121
  544.3 21.2 %convolution_add_fusion.1 = f32[256,128,128]{2,1,0:T(8,128)} fusion(f32[256,128,128]{2,1,0:T(8,128)} %fusion.120, bf16[256,64,128]{2,1,0:T(8,128)(2,1)} %copy.133, f32[128,128]{0,1:T(8,128)S(1)} %copy-done.17), kind=kOutput, calls=%fused_computation.45 | convolution fusion | flops 541097984 | bytes 37781504 | tf_op jit(solution)/shard_map/kp,bpq->bkq/dot_general | solution.py:110
  565.6 32.6 %fusion.60 = f32[256,128,128]{2,1,0:T(8,128)} fusion(f32[256,128,128]{2,1,0:T(8,128)S(1)} %convolution_add_fusion, f32[256,128,128]{2,1,0:T(8,128)} %convolution_add_fusion.1, f32[128,128]{0,1:T(8,128)S(1)} %get-tuple-element.175, f32[128,128]{0,1:T(8,128)S(1)} %get-tuple-element.176), kind=kOutput, calls=%fused_computation.112 | convolution fusion | flops 6455279616 | bytes 50462720 | tf_op jit(solution)/shard_map/bkq,ql->bkl/dot_general | solution.py:124
  598.1 32.8 %fusion.62 = f32[256,128,128]{2,1,0:T(8,128)} fusion(f32[256,128,128]{2,1,0:T(8,128)S(1)} %convolution_add_fusion, f32[256,128,128]{2,1,0:T(8,128)} %convolution_add_fusion.1, f32[128,128]{0,1:T(8,128)S(1)} %get-tuple-element.175, f32[128,128]{0,1:T(8,128)S(1)} %get-tuple-element.176), kind=kOutput, calls=%fused_computation.113 | convolution fusion | flops 6455263232 | bytes 50462720 | tf_op jit(solution)/shard_map/bkq,ql->bkl/dot_general | solution.py:121
  630.9 34.1 %convolution_subtract_fusion.2 = f32[256,128,128]{2,1,0:T(8,128)} fusion(f32[256,128,128]{2,1,0:T(8,128)} %fusion.62, f32[256,128,128]{2,1,0:T(8,128)S(1)} %convolution_add_fusion, f32[256,128,128]{2,1,0:T(8,128)} %convolution_add_fusion.1, f32[128,128]{0,1:T(8,128)S(1)} %get-tuple-element.175, f32[128,128]{0,1:T(8,128)S(1)} %get-tuple-element.176), kind=kOutput, calls=%fused_computation.51 | convolution fusion | flops 6459473920 | bytes 67239936 | tf_op jit(solution)/shard_map/bkq,ql->bkl/dot_general | solution.py:121
  665.0 51.1 %multiply_add_fusion = (f32[256,128,128]{2,1,0:T(8,128)}, f32[256,128,128]{2,1,0:T(8,128)}) fusion(f32[256,128,128]{2,1,0:T(8,128)} %convolution_subtract_fusion.1, f32[256,128,128]{2,1,0:T(8,128)} %convolution_subtract_fusion.2, f32[256,128,128]{2,1,0:T(8,128)} %convolution_add_fusion.3, f32[256,128,128]{2,1,0:T(8,128)} %fusion.60, ...), kind=kOutput, calls=%fused_computation.34 | convolution fusion | flops 6484623360 | bytes 134348800 | tf_op jit(solution)/shard_map/bkq,ql->bkl/dot_general | solution.py:124
  716.1 23.3 %fusion.85 = f32[256,128,128]{1,2,0:T(8,128)} fusion(f32[256,128,128]{2,1,0:T(8,128)} %get-tuple-element.127), kind=kOutput, calls=%fused_computation.172 | convolution fusion | flops 6442680320 | bytes 33554432 | tf_op jit(solution)/shard_map/bkl,lq->bkq/dot_general | solution.py:138
  739.4 23.0 %fusion.87 = f32[256,128,128]{1,2,0:T(8,128)} fusion(f32[256,128,128]{2,1,0:T(8,128)} %get-tuple-element.128), kind=kOutput, calls=%fused_computation.174 | convolution fusion | flops 6442680320 | bytes 33554432 | tf_op jit(solution)/shard_map/bkl,lq->bkq/dot_general | solution.py:135
  762.4 24.0 %convolution_subtract_fusion = f32[256,128,128]{1,2,0:T(8,128)} fusion(f32[256,128,128]{1,2,0:T(8,128)} %fusion.85, f32[256,128,128]{2,1,0:T(8,128)} %get-tuple-element.128), kind=kOutput, calls=%fused_computation.46 | convolution fusion | flops 6446891008 | bytes 50331648 | tf_op jit(solution)/shard_map/bkl,lq->bkq/dot_general | solution.py:138
  786.4 23.9 %convolution_add_fusion.2 = f32[256,128,128]{1,2,0:T(8,128)} fusion(f32[256,128,128]{1,2,0:T(8,128)} %fusion.87, f32[256,128,128]{2,1,0:T(8,128)} %get-tuple-element.127), kind=kOutput, calls=%fused_computation.47 | convolution fusion | flops 6446891008 | bytes 50331648 | tf_op jit(solution)/shard_map/bkl,lq->bkq/dot_general | solution.py:135
  810.3 28.7 %fusion.6 = f32[256,128,64]{1,2,0:T(8,128)} fusion(f32[256,128,128]{1,2,0:T(8,128)} %convolution_add_fusion.2, f32[256,128,128]{1,2,0:T(8,128)} %convolution_subtract_fusion, f32[128,128]{0,1:T(8,128)S(1)} %get-tuple-element.175, f32[128,128]{0,1:T(8,128)S(1)} %get-tuple-element.176, f32[128,128]{0,1:T(8,128)S(1)} %copy-done.21), kind=kOutput, calls=%fused_computation.26 | convolution fusion | flops 3233808384 | bytes 42139648 | tf_op jit(solution)/shard_map/pk,bkq->bpq/dot_general | solution.py:145
  839.0 26.8 %multiply_bitcast_fusion = f32[256,64,128]{2,1,0:T(8,128)} fusion(f32[256,128,64]{1,2,0:T(8,128)} %fusion.6, f32[256,128,128]{1,2,0:T(8,128)} %convolution_subtract_fusion, f32[256,128,128]{1,2,0:T(8,128)} %convolution_add_fusion.2, f32[128,128]{0,1:T(8,128)S(1)} %get-tuple-element.175, f32[128,128]{0,1:T(8,128)S(1)} %get-tuple-element.176, ...), kind=kOutput, calls=%fused_computation.106 | convolution fusion | flops 3238002688 | bytes 50528256 | tf_op jit(solution)/shard_map/pk,bkq->bpq/dot_general | solution.py:143
  875.2 30.1 %constant_dynamic-slice_fusion.1 = (f32[256,1,512]{2,1,0:T(1,128)}, f32[256,1,512]{2,1,0:T(1,128)}, f32[256,1,512]{2,1,0:T(1,128)}, f32[256,1,512]{2,1,0:T(1,128...) fusion(f32[256,16,512]{2,1,0:T(8,128)} %reshape_reshape.3, ...), kind=kLoop, calls=%fused_computation.220 | loop fusion | bytes 16777280 | tf_op jit(solution)/shard_map/dynamic-slice.15
  955.4 77.4 %collective-permute-done.6 = f32[256,512]{1,0:T(8,128)S(1)} collective-permute-done((f32[256,512]{1,0:T(8,128)S(1)}, f32[256,512]{1,0:T(8,128)S(1)}, u32[]{:S(2)}, u32[]{:S(2)}) %collective-permute-start.6) | collective-permute-done | bytes 524320 | tf_op jit(solution)/shard_map/ppermute | solution.py:30
  (217 shorter events, 404.8 us)
Async XLA Ops:
  38.4 196.4 %collective-permute-start = (bf16[8,3,4096]{2,0,1:T(8,128)(2,1)S(1)}, bf16[8,3,4096]{2,0,1:T(8,128)(2,1)S(1)}, u32[]{:S(2)}, u32[]{:S(2)}) collective-permute-start(bf16[8,3,4096]{2,0,1:T(8,128)(2,1)S(1)} %bitcast.336), channel_id=1, source_target_pairs={{0,2},{2,4},{4,6},{6,8},{8,10},{10,12},{12,14},{14,16},{16,18},{18... | collective-permute-start | bytes 589832 | tf_op jit(solution)/shard_map/ppermute | solution.py:38
  43.8 160.4 %copy-start.19 = (f32[128,128]{0,1:T(8,128)}, f32[128,128]{0,1:T(8,128)S(1)}, u32[]{:S(2)}) copy-start(f32[128,128]{0,1:T(8,128)S(1)} %sine_negate_fusion.1) | copy-start | bytes 196612
  314.8 3.1 collective-permute-start.1
  336.5 173.7 %all-to-all-start = ((bf16[16,256,512]{1,2,0:T(8,128)(2,1)}), bf16[16,256,512]{1,2,0:T(8,128)(2,1)}, u32[]{:S(2)}, u32[]{:S(2)}) async-start(bf16[16,256,512]{1,2,0:T(8,128)(2,1)} %bitcast.319), calls=%async_computation | async-start | bytes 8388608 | tf_op jit(solution)/shard_map/all_to_all | solution.py:196
  344.4 64.6 %slice-start = ((s8[16777216]{0:T(1024)(128)(4,1)}), s8[4194304]{0:T(1024)(128)(4,1)S(1)}, s32[]{:S(2)}) async-start(s8[16777216]{0:T(1024)(128)(4,1)} %bitcast.311), calls=%async_computation.1 | async-start | bytes 8388608
  344.4 64.6 %slice-start.1 = ((s8[16777216]{0:T(1024)(128)(4,1)}), s8[4194304]{0:T(1024)(128)(4,1)S(1)}, s32[]{:S(2)}) async-start(s8[16777216]{0:T(1024)(128)(4,1)} %bitcast.311), calls=%async_computation.2 | async-start | bytes 8388608
  476.2 40.7 %copy-start.20 = (f32[128,128]{0,1:T(8,128)S(1)}, f32[128,128]{0,1:T(8,128)}, u32[]{:S(2)}) copy-start(f32[128,128]{0,1:T(8,128)} %copy-done.19) | copy-start | bytes 196612
  544.3 86.6 %copy-start = (f32[256,128,128]{2,1,0:T(8,128)}, f32[256,128,128]{2,1,0:T(8,128)S(1)}, u32[]{:S(2)}) copy-start(f32[256,128,128]{2,1,0:T(8,128)S(1)} %convolution_add_fusion) | copy-start | bytes 50331652
  875.2 35.2 %copy-start.24 = (bf16[2,4096]{1,0:T(2,128)(2,1)S(1)}, bf16[2,4096]{1,0:T(2,128)(2,1)}, u32[]{:S(2)}) copy-start(bf16[2,4096]{1,0:T(2,128)(2,1)} %copy-done.23) | copy-start | bytes 49156
  907.7 13.1 %collective-permute-start.2 = (f32[256,512]{1,0:T(8,128)S(1)}, f32[256,512]{1,0:T(8,128)S(1)}, u32[]{:S(2)}, u32[]{:S(2)}) collective-permute-start(f32[256,512]{1,0:T(8,128)S(1)} %bitcast.335), channel_id=1, source_target_pairs={{0,2},{2,4},{4,6},{6,8},{8,10},{10,12},{12,14},{14,16},{16,18},{18... | collective-permute-start | bytes 1572872 | tf_op jit(solution)/shard_map/ppermute | solution.py:30
  909.4 22.7 %collective-permute-start.3 = (f32[256,512]{1,0:T(8,128)S(1)}, f32[256,512]{1,0:T(8,128)S(1)}, u32[]{:S(2)}, u32[]{:S(2)}) collective-permute-start(f32[256,512]{1,0:T(8,128)S(1)} %bitcast.332), channel_id=1, source_target_pairs={{0,4},{2,6},{4,8},{6,10},{8,12},{10,14},{12,16},{14,18},{16,20},{1... | collective-permute-start | bytes 1572872 | tf_op jit(solution)/shard_map/ppermute | solution.py:30
  915.1 27.8 %collective-permute-start.4 = (f32[256,512]{1,0:T(8,128)S(1)}, f32[256,512]{1,0:T(8,128)S(1)}, u32[]{:S(2)}, u32[]{:S(2)}) collective-permute-start(f32[256,512]{1,0:T(8,128)S(1)} %bitcast.333), channel_id=1, source_target_pairs={{0,6},{2,8},{4,10},{6,12},{8,14},{10,16},{12,18},{14,20},{16,22},{... | collective-permute-start | bytes 1572872 | tf_op jit(solution)/shard_map/ppermute | solution.py:30
  915.6 39.0 %collective-permute-start.5 = (f32[256,512]{1,0:T(8,128)S(1)}, f32[256,512]{1,0:T(8,128)S(1)}, u32[]{:S(2)}, u32[]{:S(2)}) collective-permute-start(f32[256,512]{1,0:T(8,128)S(1)} %bitcast.330), channel_id=1, source_target_pairs={{0,8},{2,10},{4,12},{6,14},{8,16},{10,18},{12,20},{14,22},{16,24},... | collective-permute-start | bytes 1572872 | tf_op jit(solution)/shard_map/ppermute | solution.py:30
  916.4 116.4 %collective-permute-start.6 = (f32[256,512]{1,0:T(8,128)S(1)}, f32[256,512]{1,0:T(8,128)S(1)}, u32[]{:S(2)}, u32[]{:S(2)}) collective-permute-start(f32[256,512]{1,0:T(8,128)S(1)} %bitcast.328), channel_id=1, source_target_pairs={{0,10},{2,12},{4,14},{6,16},{8,18},{10,20},{12,22},{14,24},{16,26}... | collective-permute-start | bytes 1572872 | tf_op jit(solution)/shard_map/ppermute | solution.py:30
  920.7 128.9 %collective-permute-start.7 = (f32[256,512]{1,0:T(8,128)S(1)}, f32[256,512]{1,0:T(8,128)S(1)}, u32[]{:S(2)}, u32[]{:S(2)}) collective-permute-start(f32[256,512]{1,0:T(8,128)S(1)} %bitcast.334), channel_id=1, source_target_pairs={{0,12},{2,14},{4,16},{6,18},{8,20},{10,22},{12,24},{14,26},{16,28}... | collective-permute-start | bytes 1572872 | tf_op jit(solution)/shard_map/ppermute | solution.py:30
  932.1 134.4 %collective-permute-start.8 = (f32[256,512]{1,0:T(8,128)S(1)}, f32[256,512]{1,0:T(8,128)S(1)}, u32[]{:S(2)}, u32[]{:S(2)}) collective-permute-start(f32[256,512]{1,0:T(8,128)S(1)} %bitcast.331), channel_id=1, source_target_pairs={{0,14},{2,16},{4,18},{6,20},{8,22},{10,24},{12,26},{14,28},{16,30}... | collective-permute-start | bytes 1572872 | tf_op jit(solution)/shard_map/ppermute | solution.py:30
  942.9 140.4 %collective-permute-start.9 = (f32[256,512]{1,0:T(8,128)S(1)}, f32[256,512]{1,0:T(8,128)S(1)}, u32[]{:S(2)}, u32[]{:S(2)}) collective-permute-start(f32[256,512]{1,0:T(8,128)S(1)} %bitcast.329), channel_id=1, source_target_pairs={{0,16},{2,18},{4,20},{6,22},{8,24},{10,26},{12,28},{14,30},{16,0},... | collective-permute-start | bytes 1572872 | tf_op jit(solution)/shard_map/ppermute | solution.py:30
  954.6 129.6 %collective-permute-start.10 = (f32[256,512]{1,0:T(8,128)S(1)}, f32[256,512]{1,0:T(8,128)S(1)}, u32[]{:S(2)}, u32[]{:S(2)}) collective-permute-start(f32[256,512]{1,0:T(8,128)S(1)} %bitcast.327), channel_id=1, source_target_pairs={{0,18},{2,20},{4,22},{6,24},{8,26},{10,28},{12,30},{14,0},{16,2},{... | collective-permute-start | bytes 1572872 | tf_op jit(solution)/shard_map/ppermute | solution.py:30
  1032.8 52.2 %collective-permute-start.11 = (f32[256,512]{1,0:T(8,128)S(1)}, f32[256,512]{1,0:T(8,128)S(1)}, u32[]{:S(2)}, u32[]{:S(2)}) collective-permute-start(f32[256,512]{1,0:T(8,128)S(1)} %bitcast.326), channel_id=1, source_target_pairs={{0,20},{2,22},{4,24},{6,26},{8,28},{10,30},{12,0},{14,2},{16,4},{1... | collective-permute-start | bytes 1572872 | tf_op jit(solution)/shard_map/ppermute | solution.py:30
  1049.6 36.5 %collective-permute-start.12 = (f32[256,512]{1,0:T(8,128)S(1)}, f32[256,512]{1,0:T(8,128)S(1)}, u32[]{:S(2)}, u32[]{:S(2)}) collective-permute-start(f32[256,512]{1,0:T(8,128)S(1)} %bitcast.325), channel_id=1, source_target_pairs={{0,22},{2,24},{4,26},{6,28},{8,30},{10,0},{12,2},{14,4},{16,6},{18... | collective-permute-start | bytes 1572872 | tf_op jit(solution)/shard_map/ppermute | solution.py:30
  1066.5 20.5 %collective-permute-start.13 = (f32[256,512]{1,0:T(8,128)S(1)}, f32[256,512]{1,0:T(8,128)S(1)}, u32[]{:S(2)}, u32[]{:S(2)}) collective-permute-start(f32[256,512]{1,0:T(8,128)S(1)} %bitcast.324), channel_id=1, source_target_pairs={{0,24},{2,26},{4,28},{6,30},{8,0},{10,2},{12,4},{14,6},{16,8},{18,... | collective-permute-start | bytes 1572872 | tf_op jit(solution)/shard_map/ppermute | solution.py:30
  1083.4 10.5 collective-permute-start.14
  1084.2 20.9 %collective-permute-start.15 = (f32[256,512]{1,0:T(8,128)S(1)}, f32[256,512]{1,0:T(8,128)S(1)}, u32[]{:S(2)}, u32[]{:S(2)}) collective-permute-start(f32[256,512]{1,0:T(8,128)S(1)} %bitcast.322), channel_id=1, source_target_pairs={{0,28},{2,30},{4,0},{6,2},{8,4},{10,6},{12,8},{14,10},{16,12},{18,... | collective-permute-start | bytes 1572872 | tf_op jit(solution)/shard_map/ppermute | solution.py:30
  1085.0 20.9 %collective-permute-start.16 = (f32[256,512]{1,0:T(8,128)S(1)}, f32[256,512]{1,0:T(8,128)S(1)}, u32[]{:S(2)}, u32[]{:S(2)}) collective-permute-start(f32[256,512]{1,0:T(8,128)S(1)} %bitcast.321), channel_id=1, source_target_pairs={{0,30},{2,0},{4,2},{6,4},{8,6},{10,8},{12,10},{14,12},{16,14},{18,... | collective-permute-start | bytes 1572872 | tf_op jit(solution)/shard_map/ppermute | solution.py:30
  (29 other events, 447.5 us)
